TPU v7x, 32 devices: a whole 2x2x4 slice. The times are simulated.
32 devices in a mesh: member: 16 (over z, y, x), tensor: 2 (over core).
Axes of the slice: x: 2, y: 2, z: 4, core: 2. Of those that a mesh axis runs over, the one named last changes fastest.
Arguments:
- tokens: bfloat16 [768, 5120], P('member', 'tensor'), may hold values from -6 to 6
- up_weight: bfloat16 [5120, 27648], P('tensor', 'member'), may hold values from -0.078125 to 0.078125
- left_factors: bfloat16 [192, 5120], P('member', 'tensor'), may hold values from -6 to 6
- right_factors: bfloat16 [192, 27648], P('tensor', 'member'), may hold values from -6 to 6
- fitness: float32 [48], replicated, may hold values from -0.6 to 0.6
Outputs:
- hidden: bfloat16 [768, 27648], P('tensor', 'member')
- gradient: bfloat16 [5120, 27648], P('tensor', 'member')
All inputs are finite; a program needn't handle non-finite values.
Results may differ from a plain program's by a relative error of at most 0.014.
Values may be sent and summed in bfloat16 or wider, within the bound.
A program may use at most 64 MiB of HBM per device.

v0:
```python
import jax
import jax.numpy as jnp
from jax import lax
from jax.sharding import PartitionSpec as P

D = 5120
RANK = 4
MEMBER_TOKENS = 16


def body(tokens, up_weight, left_factors, right_factors, fitness):
    noise_scale = 0.25 * D ** (-0.5)
    mixing = noise_scale * RANK ** (-0.5)
    block_span_width = tokens.shape[1]
    column_width = up_weight.shape[1]
    right_all = lax.all_gather(right_factors, "tensor", axis=0, tiled=True)
    members = right_all.shape[0] // RANK
    left_all = lax.all_gather(left_factors, "member", axis=0, tiled=True)
    all_tokens = lax.all_gather(tokens, "member", axis=0, tiled=True)
    up_projection = jnp.einsum(
        "uzg,uig->uzi",
        all_tokens.reshape(members, MEMBER_TOKENS, block_span_width),
        left_all.reshape(members, RANK, block_span_width),
        preferred_element_type=jnp.float32,
    ).astype(jnp.bfloat16)
    right_factor_grouped = right_all.reshape(members, RANK, column_width)
    base_term = jnp.dot(all_tokens, up_weight, preferred_element_type=jnp.float32)
    lowrank_correction = jnp.einsum(
        "djt,dty->djy", up_projection, right_factor_grouped, preferred_element_type=jnp.float32
    ).reshape(base_term.shape)
    summed = lax.psum_scatter(
        (base_term + mixing * lowrank_correction).astype(jnp.bfloat16),
        "tensor",
        scatter_dimension=0,
        tiled=True,
    )
    fit_rows = jnp.repeat(fitness, RANK)
    weighted = (fit_rows[:, None] * left_all.astype(jnp.float32)).astype(jnp.bfloat16)
    gradient = jnp.einsum("kd,kf->df", weighted, right_all, preferred_element_type=jnp.float32)
    gradient = gradient * (1.0 / (members * noise_scale * RANK**0.5))
    return (summed, gradient.astype(jnp.bfloat16))


def solution(mesh):
    return jax.shard_map(
        body,
        mesh=mesh,
        in_specs=(
            P("member", "tensor"),
            P("tensor", "member"),
            P("member", "tensor"),
            P("tensor", "member"),
            P(),
        ),
        out_specs=(P("tensor", "member"), P("tensor", "member")),
        check_vma=False,
    )
```

profile of v0, /device:TPU:0, one launch (start us, length us, event | category | flops | bytes accessed | tf_op | source)
XLA Modules:
  0.0 144.2 jit_solution(9186083460275813606)
XLA Ops:
  7.2 0.0 copy-start
  7.2 0.0 all-gather.3.cloned.1.call-start
  7.2 0.7 all-gather.3.cloned.1.call-update
  7.9 0.0 reduce-scatter.4.cloned.1.call-start
  8.0 56.2 %all-gather = bf16[16,12,2560]{2,1,0:T(8,128)(2,1)S(1)} all-gather(bf16[1,12,2560]{2,1,0:T(8,128)(2,1)} %bitcast.12), channel_id=1, replica_groups=mesh['member'=16,'tensor'=2] {'member'}, dimensions={0}, use_global_device_ids=true | all-gather | bytes 1044480 | tf_op jit(solution)/shard_map/all_gather | solution.py:18
  64.2 0.5 reshape.18
  64.7 0.0 copy-done
  64.7 2.3 %all_gather.11 = bf16[192,1728]{1,0:T(8,128)(2,1)S(1)} all-gather(bf16[96,1728]{1,0:T(8,128)(2,1)S(1)} %copy-done), channel_id=1, replica_groups=mesh['member'=16,'tensor'=2] {'tensor'}, dimensions={0}, use_global_device_ids=true | all-gather | bytes 995328 | tf_op jit(solution)/shard_map/all_gather | solution.py:16
  67.0 1.0 reshape.19
  68.0 27.2 %all-gather.3.cloned.1.call-done = bf16[768,2560]{1,0:T(8,128)(2,1)} async-done(((bf16[48,2560]{1,0:T(8,128)(2,1)}), bf16[768,2560]{1,0:T(8,128)(2,1)}) %all-gather.3.cloned.1.call-update) | async-done | bytes 3932176 | tf_op jit(solution)/shard_map/all_gather | solution.py:19
  95.3 7.0 %convolution_multiply_fusion = f32[48,16,1728]{2,1,0:T(8,128)} fusion(bf16[48,4,1728]{2,1,0:T(4,128)(2,1)} %reshape.19, bf16[48,16,2560]{2,1,0:T(8,128)(2,1)} %bitcast.11, bf16[48,4,2560]{2,1,0:T(4,128)(2,1)S(1)} %reshape.18), kind=kOutput, calls=%fused_computation.2 | convolution fusion | flops 27675648 | bytes 10887168 | tf_op jit(solution)/shard_map/djt,dty->djy/dot_general | solution.py:28
  102.2 6.1 %copy.9 = f32[768,1728]{0,1:T(8,128)} copy(f32[768,1728]{1,0:T(8,128)} %bitcast.10) | data formatting | bytes 10616832 | tf_op jit(solution)/shard_map/mul | solution.py:32
  108.3 12.5 %add_convert_fusion = bf16[768,1728]{0,1:T(8,128)(2,1)} fusion(f32[768,1728]{0,1:T(8,128)} %copy.9, bf16[768,2560]{1,0:T(8,128)(2,1)} %all-gather.3.cloned.1.call-done, bf16[2560,1728]{0,1:T(8,128)(2,1)} %param.6), kind=kOutput, calls=%fused_computation.1 | convolution fusion | flops 6797426688 | bytes 20742144 | tf_op jit(solution)/shard_map/dot_general | solution.py:27
  120.9 4.6 %copy.10 = bf16[768,1728]{1,0:T(8,128)(2,1)} copy(bf16[768,1728]{0,1:T(8,128)(2,1)} %add_convert_fusion) | data formatting | bytes 5308416
  125.4 0.0 copy-start.1
  125.4 0.0 reduce-scatter.4.cloned.1.call-update
  125.4 1.4 reshape.23
  126.9 0.0 copy-done.1
  126.9 0.1 broadcast_in_dim.3
  126.9 0.1 mul.28
  127.0 7.7 %multiply_convert_fusion = bf16[2560,1728]{0,1:T(8,128)(2,1)} fusion(bf16[192,1728]{1,0:T(8,128)(2,1)S(1)} %all_gather.11, f32[192,2560]{1,0:T(8,128)} %reshape.23, f32[192]{0:T(256)S(1)} %mul.28), kind=kOutput, calls=%fused_computation | convolution fusion | flops 1708523520 | bytes 11477760 | tf_op jit(solution)/shard_map/kd,kf->df/dot_general | solution.py:39
  134.7 0.1 reduce-scatter.4.cloned.1.call-done
  134.8 2.5 %copy.11 = bf16[384,1728]{0,1:T(8,128)(2,1)} copy(bf16[384,1728]{1,0:T(8,128)(2,1)} %reduce-scatter.4.cloned.1.call-done) | data formatting | bytes 2654208
Async XLA Ops:
  7.2 57.5 %copy-start = (bf16[96,1728]{1,0:T(8,128)(2,1)S(1)}, bf16[96,1728]{1,0:T(8,128)(2,1)}, u32[]{:S(2)}) copy-start(bf16[96,1728]{1,0:T(8,128)(2,1)} %param.8) | copy-start | bytes 995332
  7.2 88.1 %all-gather.3.cloned.1.call-start = ((), (), s32[]{:S(2)}) async-start(), calls=%async_computation.1 | async-start | bytes 4177920 | tf_op jit(solution)/shard_map/all_gather | solution.py:19
  7.9 126.9 %reduce-scatter.4.cloned.1.call-start = ((), (), s32[]{:S(2)}) async-start(), calls=%async_computation.2 | async-start | bytes 4128768
  125.4 1.4 %copy-start.1 = (f32[48]{0:T(128)S(1)}, f32[48]{0:T(128)}, u32[]{:S(2)}) copy-start(f32[48]{0:T(128)} %param.9) | copy-start | bytes 580
Sparse Core Ops, SparseCore 0:
  10.8 84.4 all-gather.2
  125.6 9.2 reduce-scatter.3
where the time goes:
time: 145 us; the launch traced here: 144 us
  blocking collectives  58.5 us (40%)
  waiting for transfers between devices  28 us (19%)
  matrix products  27.2 us (19%)
  local copies, waits for them, and re-layouts  16.2 us (11%)
  between operations  14.1 us (10%)
    all_gather x1, blocking collectives, body(): left_all = lax.all_gather(left_factors, 'member', axis=0, tiled=True)  56.2 us
    all_gather x1, waiting for transfers between devices, body(): all_tokens = lax.all_gather(tokens, 'member', axis=0, tiled=True)  27.2 us
    dot_general x1, matrix products, body(): jnp.dot(all_tokens, up_weight, preferred_element_type=jnp.float32)  12.5 us
    dot_general x1, matrix products, body(): jnp.einsum('kd,kf->df', weighted, right_all, preferred_element_type=jnp.f...  7.71 us
    unnamed x6, local copies, waits for them, and re-layouts  7.05 us
    dot_general x1, matrix products, body(): jnp.einsum('djt,dty->djy', up_projection, right_factor_grouped, preferred...  6.98 us
    mul x1, local copies, waits for them, and re-layouts, body(): mixing * lowrank_correction  6.09 us
  transfers between devices with their start and end apart: 2, of which 2 were waited for; matrix products, arithmetic and copies ran while one was open for 7% of the time, Pallas kernels for 0%

commit v1 on v0

v1 whole, which is shorter than its diff:
```python
import functools

import jax
import jax.numpy as jnp
from jax import lax
from jax.experimental import pallas as pl
from jax.experimental.pallas import tpu as pltpu
from jax.sharding import PartitionSpec as P

D = 5120
RANK = 4
MEMBER_TOKENS = 16
MESH = pl.DeviceIdType.MESH
NT = (((1,), (1,)), ((), ()))
TN = (((0,), (0,)), ((), ()))


def plain_body(tokens, up_weight, left_factors, right_factors, fitness):
    noise_scale = 0.25 * D ** (-0.5)
    mixing = noise_scale * RANK ** (-0.5)
    width = tokens.shape[1]
    columns = up_weight.shape[1]
    right_all = lax.all_gather(right_factors, "tensor", axis=0, tiled=True)
    members = right_all.shape[0] // RANK
    left_all = lax.all_gather(left_factors, "member", axis=0, tiled=True)
    all_tokens = lax.all_gather(tokens, "member", axis=0, tiled=True)
    projection = jnp.einsum(
        "uzg,uig->uzi",
        all_tokens.reshape(members, MEMBER_TOKENS, width),
        left_all.reshape(members, RANK, width),
        preferred_element_type=jnp.float32,
    ).astype(jnp.bfloat16)
    base = jnp.dot(all_tokens, up_weight, preferred_element_type=jnp.float32)
    correction = jnp.einsum(
        "djt,dty->djy",
        projection,
        right_all.reshape(members, RANK, columns),
        preferred_element_type=jnp.float32,
    ).reshape(base.shape)
    summed = lax.psum_scatter(
        (base + mixing * correction).astype(jnp.bfloat16), "tensor", scatter_dimension=0, tiled=True
    )
    fit_rows = jnp.repeat(fitness, RANK)
    weighted = (fit_rows[:, None] * left_all.astype(jnp.float32)).astype(jnp.bfloat16)
    gradient = jnp.einsum("kd,kf->df", weighted, right_all, preferred_element_type=jnp.float32)
    gradient = gradient * (1.0 / (members * noise_scale * RANK**0.5))
    return (summed, gradient.astype(jnp.bfloat16))


def mirror(steps):
    turn = {"u": "v", "v": "u", "x": "x", "y": "y"}
    return [
        ([(k, 3 - l) for k, l in waits], [((k, 3 - l), turn[d]) for (k, l), d in sends])
        for waits, sends in steps
    ]


def halves(l):
    return ([("x", l), ("y", l)], [(("x", l), "y"), (("y", l), "x")])


def on(l, dirs):
    return ([("c", l)], [(("c", l), d) for d in dirs])


END = [
    [halves(0), on(1, "xy"), ([("d", 0)], [(("d", 0), "u")])],
    [on(2, "xy"), on(3, "xy"), ([("x", 1), ("y", 1), ("D", 1)], [])],
    [halves(3), ([("x", 2), ("y", 2), ("D", 2)], [])],
    [([("d", 3)], [])],
]
MID = [
    [halves(1), on(0, "uxy"), on(2, "vxy"), ([("d", 1)], [])],
    [on(3, "vxy"), ([], [(("d", 1), "v"), (("d", 1), "u")]), ([("x", 0), ("y", 0), ("D", 0)], [])],
    [([("x", 2), ("y", 2)], []), ([("D", 2)], [(("D", 2), "v")]), halves(3)],
    [([("d", 3)], [])],
]
PLAN = [END, MID, [mirror(s) for s in MID], [mirror(s) for s in END]]
ORDER = [[0, 1, 2, 3], [1, 0, 2, 3], [2, 3, 1, 0], [3, 2, 1, 0]]


def tile_of(n, step, most):
    best = step
    for size in range(step, most + 1, step):
        if n % size == 0:
            best = size
    return best


def gather_kernel(
    mixing, tok_in, w_in, left_in, right_in,
    rt_ref, lpad_ref, own_ref, got_ref,
    tok, left, w, rall, sendb,
    send_sem, recv_sem, local_sem, w_sem, r_send, r_recv, p_send, p_recv,
):
    m = lax.axis_index("member")
    t = lax.axis_index("tensor")
    z, y, x = m // 4, (m // 2) % 2, m % 2
    width = tok_in.shape[1]
    half = width // 2
    rows = tok_in.shape[0]
    pad = lpad_ref.shape[0] // 16
    facts = left_in.shape[0]
    ftotal = w.shape[0]

    def at(l, yy, xx):
        return 4 * l + 2 * yy + xx

    def member_of(kind, l):
        if kind == "c":
            return at(l, y, x)
        if kind == "x":
            return at(l, y, 1 - x)
        if kind == "y":
            return at(l, 1 - y, x)
        return at(l, 1 - y, 1 - x)

    barrier = pltpu.get_barrier_semaphore()
    for peer in (at(z, y, 1 - x), at(z, 1 - y, x)):
        pl.semaphore_signal(barrier, inc=1, device_id=(peer, t), device_id_type=MESH)
    pl.semaphore_signal(barrier, inc=1, device_id=(m, 1 - t), device_id_type=MESH)

    @pl.when(z > 0)
    def _():
        pl.semaphore_signal(barrier, inc=1, device_id=(m - 4, t), device_id_type=MESH)

    @pl.when(z < 3)
    def _():
        pl.semaphore_signal(barrier, inc=1, device_id=(m + 4, t), device_id_type=MESH)

    local = [
        pltpu.make_async_copy(tok_in, tok.at[m], local_sem.at[0]),
        pltpu.make_async_copy(left_in, left.at[m], local_sem.at[1]),
        pltpu.make_async_copy(right_in, rall.at[t], local_sem.at[2]),
        pltpu.make_async_copy(w_in, w, w_sem),
    ]
    for copy in local:
        copy.start()

    @pl.when((z == 0) | (z == 3))
    def _():
        pl.semaphore_wait(barrier, 4)

    @pl.when((z == 1) | (z == 2))
    def _():
        pl.semaphore_wait(barrier, 5)

    bufs = (tok, left)

    def peer_of(direction, plane):
        if direction == "x":
            return at(plane, y, 1 - x)
        if direction == "y":
            return at(plane, 1 - y, x)
        return at(plane + (1 if direction == "u" else -1), y, x)

    def copies(item, direction, plane, slot):
        kind, l = item
        own = kind == "c" and l == plane
        who = member_of(kind, l)
        out = []
        cut = kind in "xy"
        part = 0 if direction == "y" else 1
        for b, buf in enumerate(bufs):
            src = (tok_in, left_in)[b] if own else buf.at[who]
            dst = buf.at[who]
            if cut:
                src = src.at[:, pl.ds(part * half, half)]
                dst = dst.at[:, pl.ds(part * half, half)]
            out.append(
                pltpu.make_async_remote_copy(
                    src_ref=src,
                    dst_ref=dst,
                    send_sem=send_sem.at[b, slot],
                    recv_sem=recv_sem.at[b, who, part if cut else 0],
                    device_id=(peer_of(direction, plane), t),
                    device_id_type=MESH,
                )
            )
        return out

    def await_item(item):
        kind, l = item
        who = member_of(kind, l)
        for b, buf in enumerate(bufs):
            if kind == "d":
                for part in range(2):
                    piece = buf.at[who, :, pl.ds(part * half, half)]
                    pltpu.make_async_copy(piece, piece, recv_sem.at[b, who, part]).wait()
            else:
                pltpu.make_async_copy(buf.at[who], buf.at[who], recv_sem.at[b, who, 0]).wait()

    started = {k: [] for k in range(4)}

    def send(item, direction, plane):
        pair = copies(item, direction, plane, len(started[plane]))
        started[plane].append((item, direction))
        for copy in pair:
            copy.start()

    for plane in range(4):
        @pl.when(z == plane)
        def _(plane=plane):
            dirs = {0: "uxy", 3: "vxy"}.get(plane, "uvxy")
            for d in dirs:
                send(("c", plane), d, plane)

    r_copy = pltpu.make_async_remote_copy(
        src_ref=right_in, dst_ref=rall.at[t], send_sem=r_send, recv_sem=r_recv,
        device_id=(m, 1 - t), device_id_type=MESH,
    )
    r_copy.start()

    lpad_ref[...] = jnp.zeros_like(lpad_ref)
    kk = lax.broadcasted_iota(jnp.int32, (2 * rall.shape[1], 16 * pad), 0)
    qq = lax.broadcasted_iota(jnp.int32, (2 * rall.shape[1], 16 * pad), 1)
    slot_q = qq % pad
    spread = jnp.where((slot_q < facts) & (kk == facts * (qq // pad) + slot_q), 1.0, 0.0)
    spread = spread.astype(jnp.bfloat16)
    local[2].wait()
    r_copy.wait()
    r_val = jnp.concatenate([rall[0], rall[1]], axis=0)
    rt_ref[...] = lax.dot_general(
        r_val, spread, TN, preferred_element_type=jnp.float32
    ).astype(jnp.bfloat16)
    local[0].wait()
    local[1].wait()

    ft = tile_of(ftotal, 16, 448)

    def layer_index(step):
        ind = 0
        for plane in range(4):
            ind = ind + jnp.where(z == plane, ORDER[plane][step], 0)
        return ind

    def compute(l, out_ref):
        side = l % 2
        for i in range(4):
            lv = left[4 * l + i]
            if facts < pad:
                lv = jnp.concatenate([lv, jnp.zeros((pad - facts, width), lv.dtype)], axis=0)
            lpad_ref[pl.ds(pl.multiple_of((4 * l + i) * pad, 16), pad), :] = lv
        toks = tok[pl.ds(4 * l, 4)].reshape(4 * rows, width)
        proj = lax.dot_general(toks, lpad_ref[...], NT, preferred_element_type=jnp.float32)
        rr = lax.broadcasted_iota(jnp.int32, proj.shape, 0)
        qc = lax.broadcasted_iota(jnp.int32, proj.shape, 1)
        sq = qc % pad
        mine = (sq < facts) & (
            (facts // RANK) * (qc // pad) + sq // RANK == (4 * rows // MEMBER_TOKENS) * l + rr // MEMBER_TOKENS
        )
        proj = jnp.where(mine, proj, 0.0).astype(jnp.bfloat16)

        @pl.loop(0, ftotal // ft)
        def _(i):
            span = pl.ds(pl.multiple_of(i * ft, 16), ft)
            value = lax.dot_general(
                w[span, :], tok[pl.ds(4 * l, 4)].reshape(4 * rows, width), NT,
                preferred_element_type=jnp.float32,
            )
            value = value + mixing * lax.dot_general(
                rt_ref[span, :], proj, NT, preferred_element_type=jnp.float32
            )
            out_ref[side, span, :] = value.astype(jnp.bfloat16)

    def exchange(side):
        return pltpu.make_async_remote_copy(
            src_ref=sendb.at[side], dst_ref=got_ref.at[side],
            send_sem=p_send.at[side], recv_sem=p_recv.at[side],
            device_id=(m, 1 - t), device_id_type=MESH,
        )

    for step in range(4):
        for plane in range(4):
            @pl.when(z == plane)
            def _(plane=plane, step=step):
                for waits, sends in PLAN[plane][step]:
                    for item in waits:
                        await_item(item)
                    for item, d in sends:
                        send(item, d, plane)
        l = layer_index(step)
        if step == 0:
            local[3].wait()

        @pl.when(l // 2 == t)
        def _():
            compute(l, own_ref)

        @pl.when(l // 2 != t)
        def _():
            compute(l, sendb)
            exchange(l % 2).start()

    for plane in range(4):
        @pl.when(z == plane)
        def _(plane=plane):
            for slot, (item, d) in enumerate(started[plane]):
                for copy in copies(item, d, plane, slot):
                    copy.wait_send()
    for side in range(2):
        exchange(side).wait()


def finish_kernel(scale, facts, fit_ref, lpad_ref, rt_ref, own_ref, got_ref, h_ref, g_ref, wl):
    pad = wl.shape[0] // 16

    @pl.when(pl.program_id(0) == 0)
    def _():
        for b in range(16):
            rows = lax.broadcasted_iota(jnp.int32, (pad, 1), 0) // RANK
            col = jnp.zeros((pad, 1), jnp.float32)
            for j in range(facts // RANK):
                col = jnp.where(rows == j, fit_ref[b * (facts // RANK) + j], col)
            part = lpad_ref[pl.ds(b * pad, pad), :].astype(jnp.float32) * col
            wl[pl.ds(b * pad, pad), :] = part.astype(jnp.bfloat16)

    n = own_ref.shape[2]
    for side in range(2):
        total = own_ref[side].astype(jnp.float32) + got_ref[side].astype(jnp.float32)
        h_ref[:, side * n:(side + 1) * n] = total.astype(jnp.bfloat16)
    g = jnp.dot(rt_ref[...], wl[...], preferred_element_type=jnp.float32)
    g_ref[...] = (g * scale).astype(jnp.bfloat16)


def body(tokens, up_weight, left_factors, right_factors, fitness):
    noise_scale = 0.25 * D ** (-0.5)
    mixing = noise_scale * RANK ** (-0.5)
    rows, width = tokens.shape
    facts = left_factors.shape[0]
    columns = up_weight.shape[1]
    rrows = right_factors.shape[0]
    pad = -(-facts // 16) * 16
    members = fitness.shape[0]
    bf = jnp.bfloat16
    anyspec = pl.BlockSpec(memory_space=pl.ANY)
    vm = pl.BlockSpec(memory_space=pltpu.VMEM)
    dma = pltpu.SemaphoreType.DMA
    nsend = 24
    part = jax.ShapeDtypeStruct((2, columns, 4 * rows), bf)
    rt, lpad, own, got = pl.pallas_call(
        functools.partial(gather_kernel, mixing),
        out_shape=(
            jax.ShapeDtypeStruct((columns, 16 * pad), bf),
            jax.ShapeDtypeStruct((16 * pad, width), bf),
            part,
            part,
        ),
        in_specs=[anyspec] * 4,
        out_specs=(vm, vm, vm, vm),
        scratch_shapes=[
            pltpu.VMEM((16, rows, width), bf),
            pltpu.VMEM((16, facts, width), bf),
            pltpu.VMEM((columns, width), bf),
            pltpu.VMEM((2, rrows, columns), bf),
            pltpu.VMEM((2, columns, 4 * rows), bf),
            dma((2, nsend)), dma((2, 16, 2)), dma((3,)), dma, dma, dma, dma((2,)), dma((2,)),
        ],
        compiler_params=pltpu.CompilerParams(
            collective_id=0, has_side_effects=True, vmem_limit_bytes=40 * 1024 * 1024
        ),
        name="gather_project",
    )(tokens, up_weight.T, left_factors, right_factors)

    tf = tile_of(columns, 16, 192)
    hidden, gradient = pl.pallas_call(
        functools.partial(finish_kernel, 1.0 / (members * noise_scale * RANK**0.5), facts),
        grid=(columns // tf,),
        out_shape=(
            jax.ShapeDtypeStruct((columns, 8 * rows), bf),
            jax.ShapeDtypeStruct((columns, width), bf),
        ),
        in_specs=[
            pl.BlockSpec(memory_space=pltpu.SMEM),
            pl.BlockSpec((16 * pad, width), lambda i: (0, 0)),
            pl.BlockSpec((tf, 16 * pad), lambda i: (i, 0)),
            pl.BlockSpec((2, tf, 4 * rows), lambda i: (0, i, 0)),
            pl.BlockSpec((2, tf, 4 * rows), lambda i: (0, i, 0)),
        ],
        out_specs=(
            pl.BlockSpec((tf, 8 * rows), lambda i: (i, 0)),
            pl.BlockSpec((tf, width), lambda i: (i, 0)),
        ),
        scratch_shapes=[pltpu.VMEM((16 * pad, width), bf)],
        compiler_params=pltpu.CompilerParams(vmem_limit_bytes=24 * 1024 * 1024),
        name="finish",
    )(fitness, lpad, rt, own, got)
    return hidden.T, gradient.T


def solution(mesh):
    fits = mesh.shape["member"] == 16 and mesh.shape["tensor"] == 2
    return jax.shard_map(
        body if fits else plain_body,
        mesh=mesh,
        in_specs=(
            P("member", "tensor"),
            P("tensor", "member"),
            P("member", "tensor"),
            P("tensor", "member"),
            P(),
        ),
        out_specs=(P("tensor", "member"), P("tensor", "member")),
        check_vma=False,
    )
```

time: 145 us -> 65.8 us (0.45)
  Pallas kernels: 0 us -> 62.1 us
  blocking collectives: 58.5 us -> 0 us
  waiting for transfers between devices: 28 us -> 0 us
  matrix products: 27.2 us -> 0 us
  between operations: 14.1 us -> 0.66 us
  local copies, waits for them, and re-layouts: 16.2 us -> 2.81 us
    pallas_call x0 -> x2, Pallas kernels: none -> 62.1 us  [the longest x1 54.3 us: body(): pl.pallas_call(functools.partial(gather_kernel, mixing), out_shape=(jax.S...]
    all_gather x2 -> x0, blocking collectives: 58.5 us -> none  [the longest x1 56.2 us: body(): left_all = lax.all_gather(left_factors, 'member', axis=0, tiled=True)]
    all_gather x1 -> x0, waiting for transfers between devices: 27.2 us -> none  [body(): all_tokens = lax.all_gather(tokens, 'member', axis=0, tiled=True)]
    dot_general x3 -> x0, matrix products: 27.2 us -> none  [the longest x1 12.5 us: body(): jnp.dot(all_tokens, up_weight, preferred_element_type=jnp.float32)]
    mul x2 -> x0, local copies, waits for them, and re-layouts: 6.19 us -> none  [the longest x1 6.09 us: body(): mixing * lowrank_correction]
    unnamed x6 -> x8, local copies, waits for them, and re-layouts: 7.05 us -> 2.81 us
    reshape x2 -> x0, local copies, waits for them, and re-layouts: 1.51 us -> none  [the longest x1 1.01 us: body(): right_factor_grouped = right_all.reshape(members, RANK, column_width)]
  transfers between devices with their start and end apart: 2 -> 0, of which waited for: 2 -> 0; matrix products, arithmetic and copies ran while one was open for 7% -> 0% of each run, Pallas kernels for 0% -> 0%
where the time goes in v1:
time: 65.8 us; the launch traced here: 65.6 us
  Pallas kernels  62.1 us (94%)
  local copies, waits for them, and re-layouts  2.81 us (4%)
  between operations  0.66 us (1%)
    pallas_call x1, Pallas kernels, body(): pl.pallas_call(functools.partial(gather_kernel, mixing), out_shape=(jax.S...  54.3 us
    pallas_call x1, Pallas kernels, body(): pl.pallas_call(functools.partial(finish_kernel, 1.0 / (members * noise_sc...  7.83 us
    unnamed x8, local copies, waits for them, and re-layouts  2.81 us

profile of v1, /device:TPU:0, one launch (start us, length us, event | category | flops | bytes accessed | tf_op | source)
XLA Modules:
  0.0 65.6 jit_solution(18161235043784324080)
XLA Ops:
  0.6 0.0 copy-start
  0.6 1.0 %copy-done = bf16[96,1728]{1,0:T(8,128)(2,1)S(1)} copy-done((bf16[96,1728]{1,0:T(8,128)(2,1)S(1)}, bf16[96,1728]{1,0:T(8,128)(2,1)}, u32[]{:S(2)}) %copy-start) | copy-done | bytes 331800
  1.6 0.0 copy-start.1
  1.6 0.9 %copy-done.1 = bf16[48,2560]{1,0:T(8,128)(2,1)S(1)} copy-done((bf16[48,2560]{1,0:T(8,128)(2,1)S(1)}, bf16[48,2560]{1,0:T(8,128)(2,1)}, u32[]{:S(2)}) %copy-start.1) | copy-done | bytes 245784
  2.6 0.0 copy-start.2
  2.6 0.9 %copy-done.2 = bf16[12,2560]{1,0:T(8,128)(2,1)S(1)} copy-done((bf16[12,2560]{1,0:T(8,128)(2,1)S(1)}, bf16[12,2560]{1,0:T(8,128)(2,1)}, u32[]{:S(2)}) %copy-start.2) | copy-done | bytes 61464
  3.4 0.0 copy-start.3
  3.4 54.3 %gather_project.1 = (bf16[1728,256]{1,0:T(8,128)(2,1)S(1)}, bf16[256,2560]{1,0:T(8,128)(2,1)S(1)}, bf16[2,1728,192]{2,1,0:T(8,128)(2,1)S(1)}, bf16[2,1728,192]{2,1,0:T(8,128)(2,1)S(1)}) custom-call(bf16[48,2560]{1,0:T(8,128)(2,1)S(1)} %copy-done.1, bf16[1728,2560]{1,0:T(8,128)(2,1)} %bitcast.3, bf16[12,2560]{1,0:T(8,128)(2,1)S(1)} %copy-done.2, ...), custom_call_target="tpu_custom_call" | custom-call | tf_op jit(solution)/shard_map/gather_project/pallas_call | solution.py:341
  57.7 0.0 copy-done.3
  57.7 7.8 %finish.1 = (bf16[1728,384]{1,0:T(8,128)(2,1)}, bf16[1728,2560]{1,0:T(8,128)(2,1)}) custom-call(f32[48]{0:T(128)S(1)} %copy-done.3, bf16[256,2560]{1,0:T(8,128)(2,1)S(1)} %get-tuple-element.8.lpad_ref, bf16[1728,256]{1,0:T(8,128)(2,1)S(1)} %get-tuple-element.9.rt_ref, bf16[2,1728,192]{2,1,0:T(8,128)(2,1)S(1)} %get-tuple-element.10.own_ref, ...), custom_call_target="tpu_custom_call" | custom-call | tf_op jit(solution)/shard_map/finish/pallas_call | solution.py:366
Async XLA Ops:
  0.6 1.0 %copy-start = (bf16[96,1728]{1,0:T(8,128)(2,1)S(1)}, bf16[96,1728]{1,0:T(8,128)(2,1)}, u32[]{:S(2)}) copy-start(bf16[96,1728]{1,0:T(8,128)(2,1)} %right_in.1) | copy-start | bytes 995332
  1.6 0.9 %copy-start.1 = (bf16[48,2560]{1,0:T(8,128)(2,1)S(1)}, bf16[48,2560]{1,0:T(8,128)(2,1)}, u32[]{:S(2)}) copy-start(bf16[48,2560]{1,0:T(8,128)(2,1)} %tok_in.1) | copy-start | bytes 737284
  2.6 0.9 %copy-start.2 = (bf16[12,2560]{1,0:T(8,128)(2,1)S(1)}, bf16[12,2560]{1,0:T(8,128)(2,1)}, u32[]{:S(2)}) copy-start(bf16[12,2560]{1,0:T(8,128)(2,1)} %left_in.1) | copy-start | bytes 184324
  3.4 54.3 %copy-start.3 = (f32[48]{0:T(128)S(1)}, f32[48]{0:T(128)}, u32[]{:S(2)}) copy-start(f32[48]{0:T(128)} %fit_ref.1) | copy-start | bytes 580

commit v2 on v1

--- a/solution.py
+++ b/solution.py
@@ -65,15 +65,15 @@
 
 END = [
     [halves(0), on(1, "xy"), ([("d", 0)], [(("d", 0), "u")])],
-    [on(2, "xy"), on(3, "xy"), ([("x", 1), ("y", 1), ("D", 1)], [])],
-    [halves(3), ([("x", 2), ("y", 2), ("D", 2)], [])],
-    [([("d", 3)], [])],
+    [on(2, "xy"), ([("x", 1), ("y", 1), ("D", 1)], [])],
+    [halves(2), on(3, "xy"), ([("d", 2)], [])],
+    [([("x", 3), ("y", 3), ("D", 3)], [])],
 ]
 MID = [
-    [halves(1), on(0, "uxy"), on(2, "vxy"), ([("d", 1)], [])],
-    [on(3, "vxy"), ([], [(("d", 1), "v"), (("d", 1), "u")]), ([("x", 0), ("y", 0), ("D", 0)], [])],
-    [([("x", 2), ("y", 2)], []), ([("D", 2)], [(("D", 2), "v")]), halves(3)],
-    [([("d", 3)], [])],
+    [halves(1), on(0, "uxy"), on(2, "vxy"), ([("d", 1)], [(("d", 1), "v")])],
+    [on(3, "v"), ([("x", 0), ("y", 0), ("D", 0)], [(("D", 0), "u")])],
+    [halves(2), ([], [(("c", 3), "x"), (("c", 3), "y")]), ([("D", 3)], [(("D", 3), "v")]), ([("d", 2)], [])],
+    [([("x", 3), ("y", 3)], [])],
 ]
 PLAN = [END, MID, [mirror(s) for s in MID], [mirror(s) for s in END]]
 ORDER = [[0, 1, 2, 3], [1, 0, 2, 3], [2, 3, 1, 0], [3, 2, 1, 0]]
@@ -302,25 +302,21 @@
         exchange(side).wait()
 
 
-def finish_kernel(scale, facts, fit_ref, lpad_ref, rt_ref, own_ref, got_ref, h_ref, g_ref, wl):
-    pad = wl.shape[0] // 16
-
-    @pl.when(pl.program_id(0) == 0)
-    def _():
-        for b in range(16):
-            rows = lax.broadcasted_iota(jnp.int32, (pad, 1), 0) // RANK
-            col = jnp.zeros((pad, 1), jnp.float32)
-            for j in range(facts // RANK):
-                col = jnp.where(rows == j, fit_ref[b * (facts // RANK) + j], col)
-            part = lpad_ref[pl.ds(b * pad, pad), :].astype(jnp.float32) * col
-            wl[pl.ds(b * pad, pad), :] = part.astype(jnp.bfloat16)
-
+def finish_kernel(scale, facts, fit_ref, lpad_ref, rt_ref, own_ref, got_ref, h_ref, g_ref):
+    pad = lpad_ref.shape[0] // 16
+    rows = lax.broadcasted_iota(jnp.int32, (pad, 1), 0) // RANK
+    parts = []
+    for b in range(16):
+        col = jnp.zeros((pad, 1), jnp.float32)
+        for j in range(facts // RANK):
+            col = jnp.where(rows == j, fit_ref[b * (facts // RANK) + j], col)
+        parts.append((lpad_ref[pl.ds(b * pad, pad), :].astype(jnp.float32) * col).astype(jnp.bfloat16))
+    g = jnp.dot(rt_ref[...], jnp.concatenate(parts, axis=0), preferred_element_type=jnp.float32)
+    g_ref[...] = (g * scale).astype(jnp.bfloat16)
     n = own_ref.shape[2]
     for side in range(2):
         total = own_ref[side].astype(jnp.float32) + got_ref[side].astype(jnp.float32)
         h_ref[:, side * n:(side + 1) * n] = total.astype(jnp.bfloat16)
-    g = jnp.dot(rt_ref[...], wl[...], preferred_element_type=jnp.float32)
-    g_ref[...] = (g * scale).astype(jnp.bfloat16)
 
 
 def body(tokens, up_weight, left_factors, right_factors, fitness):
@@ -333,7 +329,7 @@
     pad = -(-facts // 16) * 16
     members = fitness.shape[0]
     bf = jnp.bfloat16
-    anyspec = pl.BlockSpec(memory_space=pl.ANY)
+    anyspec = pl.BlockSpec(memory_space=pltpu.HBM)
     vm = pl.BlockSpec(memory_space=pltpu.VMEM)
     dma = pltpu.SemaphoreType.DMA
     nsend = 24
@@ -360,28 +356,35 @@
             collective_id=0, has_side_effects=True, vmem_limit_bytes=40 * 1024 * 1024
         ),
         name="gather_project",
-    )(tokens, up_weight.T, left_factors, right_factors)
+    )(
+        pltpu.with_memory_space_constraint(tokens, pltpu.HBM),
+        pltpu.with_memory_space_constraint(up_weight.T, pltpu.HBM),
+        pltpu.with_memory_space_constraint(left_factors, pltpu.HBM),
+        pltpu.with_memory_space_constraint(right_factors, pltpu.HBM),
+    )
 
     tf = tile_of(columns, 16, 192)
+    td = tile_of(width, 128, 256)
+    steps = max(width // td, columns // tf)
+    last_f, last_d = columns // tf - 1, width // td - 1
     hidden, gradient = pl.pallas_call(
         functools.partial(finish_kernel, 1.0 / (members * noise_scale * RANK**0.5), facts),
-        grid=(columns // tf,),
+        grid=(steps,),
         out_shape=(
             jax.ShapeDtypeStruct((columns, 8 * rows), bf),
             jax.ShapeDtypeStruct((columns, width), bf),
         ),
         in_specs=[
             pl.BlockSpec(memory_space=pltpu.SMEM),
-            pl.BlockSpec((16 * pad, width), lambda i: (0, 0)),
-            pl.BlockSpec((tf, 16 * pad), lambda i: (i, 0)),
-            pl.BlockSpec((2, tf, 4 * rows), lambda i: (0, i, 0)),
-            pl.BlockSpec((2, tf, 4 * rows), lambda i: (0, i, 0)),
+            pl.BlockSpec((16 * pad, td), lambda i: (0, jnp.minimum(i, last_d))),
+            pl.BlockSpec((columns, 16 * pad), lambda i: (0, 0)),
+            pl.BlockSpec((2, tf, 4 * rows), lambda i: (0, jnp.minimum(i, last_f), 0)),
+            pl.BlockSpec((2, tf, 4 * rows), lambda i: (0, jnp.minimum(i, last_f), 0)),
         ],
         out_specs=(
-            pl.BlockSpec((tf, 8 * rows), lambda i: (i, 0)),
-            pl.BlockSpec((tf, width), lambda i: (i, 0)),
+            pl.BlockSpec((tf, 8 * rows), lambda i: (jnp.minimum(i, last_f), 0)),
+            pl.BlockSpec((columns, td), lambda i: (0, jnp.minimum(i, last_d))),
         ),
-        scratch_shapes=[pltpu.VMEM((16 * pad, width), bf)],
         compiler_params=pltpu.CompilerParams(vmem_limit_bytes=24 * 1024 * 1024),
         name="finish",
     )(fitness, lpad, rt, own, got)

time: 65.8 us -> 60.1 us (0.913)
  Pallas kernels: 62.1 us -> 59.3 us
  local copies, waits for them, and re-layouts: 2.81 us -> 0.01 us
    pallas_call x1, Pallas kernels: 54.3 us -> 51.4 us  [body(): pl.pallas_call(functools.partial(gather_kernel, mixing), out_shape=(jax.S...]
    unnamed x8 -> x2, local copies, waits for them, and re-layouts: 2.81 us -> 0.01 us
where the time goes in v2:
time: 60.1 us; the launch traced here: 59.9 us
  Pallas kernels  59.3 us (99%)
  between operations  0.65 us (1%)
    pallas_call x1, Pallas kernels, body(): pl.pallas_call(functools.partial(gather_kernel, mixing), out_shape=(jax.S...  51.4 us
    pallas_call x1, Pallas kernels, body(): pl.pallas_call(functools.partial(finish_kernel, 1.0 / (members * noise_sc...  7.86 us

profile of v2, /device:TPU:0, one launch (start us, length us, event | category | flops | bytes accessed | tf_op | source)
XLA Modules:
  0.0 59.9 jit_solution(1048514020380492115)
XLA Ops:
  0.6 0.0 copy-start
  0.6 51.4 %gather_project.1 = (bf16[1728,256]{1,0:T(8,128)(2,1)S(1)}, bf16[256,2560]{1,0:T(8,128)(2,1)S(1)}, bf16[2,1728,192]{2,1,0:T(8,128)(2,1)S(1)}, bf16[2,1728,192]{2,1,0:T(8,128)(2,1)S(1)}) custom-call(bf16[48,2560]{1,0:T(8,128)(2,1)} %tok_in.1, bf16[1728,2560]{1,0:T(8,128)(2,1)} %bitcast.3, bf16[12,2560]{1,0:T(8,128)(2,1)} %left_in.1, bf16[96,1728]{1,0:T(8,128)(2,1)} %right_in.1), custom_call_target="tpu_custom_call" | custom-call | tf_op jit(solution)/shard_map/gather_project/pallas_call | solution.py:337
  52.1 0.0 copy-done
  52.1 7.9 %finish.1 = (bf16[1728,384]{1,0:T(8,128)(2,1)}, bf16[1728,2560]{1,0:T(8,128)(2,1)}) custom-call(f32[48]{0:T(128)S(1)} %copy-done, bf16[256,2560]{1,0:T(8,128)(2,1)S(1)} %get-tuple-element.8.lpad_ref, bf16[1728,256]{1,0:T(8,128)(2,1)S(1)} %get-tuple-element.9.rt_ref, bf16[2,1728,192]{2,1,0:T(8,128)(2,1)S(1)} %get-tuple-element.10.own_ref, ...), custom_call_target="tpu_custom_call" | custom-call | tf_op jit(solution)/shard_map/finish/pallas_call | solution.py:370
Async XLA Ops:
  0.6 51.4 %copy-start = (f32[48]{0:T(128)S(1)}, f32[48]{0:T(128)}, u32[]{:S(2)}) copy-start(f32[48]{0:T(128)} %fit_ref.1) | copy-start | bytes 580

commit v3 on v2

--- a/solution.py
+++ b/solution.py
@@ -47,33 +47,38 @@
     return (summed, gradient.astype(jnp.bfloat16))
 
 
-def mirror(steps):
-    turn = {"u": "v", "v": "u", "x": "x", "y": "y"}
-    return [
-        ([(k, 3 - l) for k, l in waits], [((k, 3 - l), turn[d]) for (k, l), d in sends])
-        for waits, sends in steps
-    ]
-
-
-def halves(l):
-    return ([("x", l), ("y", l)], [(("x", l), "y"), (("y", l), "x")])
-
-
-def on(l, dirs):
-    return ([("c", l)], [(("c", l), d) for d in dirs])
+def mirror(step):
+    turn = str.maketrans("uv", "vu")
+    return [(k, 3 - l, p, dirs.translate(turn)) for k, l, p, dirs in step]
 
 
 END = [
-    [halves(0), on(1, "xy"), ([("d", 0)], [(("d", 0), "u")])],
-    [on(2, "xy"), ([("x", 1), ("y", 1), ("D", 1)], [])],
-    [halves(2), on(3, "xy"), ([("d", 2)], [])],
-    [([("x", 3), ("y", 3), ("D", 3)], [])],
+    [
+        ("x", 0, 0, "y"), ("y", 0, 1, "x"), ("c", 1, 0, "xy"), ("c", 1, 1, "xy"),
+        ("d", 0, 0, "u"), ("d", 0, 1, "u"),
+    ],
+    [
+        ("c", 2, 0, "xy"), ("c", 2, 1, "xy"), ("c", 3, 0, "xy"),
+        ("x", 2, 0, "y"), ("y", 2, 1, "x"), ("c", 3, 1, "xy"),
+    ],
+    [],
+    [],
 ]
 MID = [
-    [halves(1), on(0, "uxy"), on(2, "vxy"), ([("d", 1)], [(("d", 1), "v")])],
-    [on(3, "v"), ([("x", 0), ("y", 0), ("D", 0)], [(("D", 0), "u")])],
-    [halves(2), ([], [(("c", 3), "x"), (("c", 3), "y")]), ([("D", 3)], [(("D", 3), "v")]), ([("d", 2)], [])],
-    [([("x", 3), ("y", 3)], [])],
+    [
+        ("c", 2, 0, "v"), ("c", 0, 0, "u"), ("x", 1, 0, "y"), ("y", 1, 1, "x"),
+        ("c", 0, 0, "xy"), ("c", 2, 1, "v"), ("c", 0, 1, "u"), ("c", 0, 1, "xy"),
+        ("c", 2, 0, "xy"), ("c", 2, 1, "xy"), ("c", 3, 0, "v"),
+    ],
+    [
+        ("c", 3, 1, "v"), ("d", 1, 0, "v"), ("d", 1, 1, "v"),
+        ("d", 0, 0, "u"), ("d", 0, 1, "u"),
+    ],
+    [
+        ("x", 2, 0, "y"), ("c", 3, 0, "xy"), ("d", 3, 0, "v"), ("y", 2, 1, "x"),
+        ("c", 3, 1, "xy"), ("d", 3, 1, "v"),
+    ],
+    [],
 ]
 PLAN = [END, MID, [mirror(s) for s in MID], [mirror(s) for s in END]]
 ORDER = [[0, 1, 2, 3], [1, 0, 2, 3], [2, 3, 1, 0], [3, 2, 1, 0]]
@@ -154,56 +159,46 @@
             return at(plane, 1 - y, x)
         return at(plane + (1 if direction == "u" else -1), y, x)
 
-    def copies(item, direction, plane, slot):
-        kind, l = item
-        own = kind == "c" and l == plane
+    def copies(event, plane, slot):
+        kind, l, part, direction = event
         who = member_of(kind, l)
-        out = []
-        cut = kind in "xy"
-        part = 0 if direction == "y" else 1
-        for b, buf in enumerate(bufs):
-            src = (tok_in, left_in)[b] if own else buf.at[who]
-            dst = buf.at[who]
-            if cut:
-                src = src.at[:, pl.ds(part * half, half)]
-                dst = dst.at[:, pl.ds(part * half, half)]
-            out.append(
-                pltpu.make_async_remote_copy(
-                    src_ref=src,
-                    dst_ref=dst,
-                    send_sem=send_sem.at[b, slot],
-                    recv_sem=recv_sem.at[b, who, part if cut else 0],
-                    device_id=(peer_of(direction, plane), t),
-                    device_id_type=MESH,
-                )
+        span = pl.ds(part * half, half)
+        return [
+            pltpu.make_async_remote_copy(
+                src_ref=((tok_in, left_in)[b] if kind == "c" and l == plane else buf.at[who]).at[:, span],
+                dst_ref=buf.at[who].at[:, span],
+                send_sem=send_sem.at[b, slot],
+                recv_sem=recv_sem.at[b, who, part],
+                device_id=(peer_of(direction, plane), t),
+                device_id_type=MESH,
             )
-        return out
-
-    def await_item(item):
-        kind, l = item
+            for b, buf in enumerate(bufs)
+        ]
+
+    started = {k: [] for k in range(4)}
+    waited = {k: set() for k in range(4)}
+
+    def arrive(plane, kind, l, part):
+        if (kind, l) == ("c", plane) or (kind, l, part) in waited[plane]:
+            return
+        waited[plane].add((kind, l, part))
         who = member_of(kind, l)
         for b, buf in enumerate(bufs):
-            if kind == "d":
-                for part in range(2):
-                    piece = buf.at[who, :, pl.ds(part * half, half)]
-                    pltpu.make_async_copy(piece, piece, recv_sem.at[b, who, part]).wait()
-            else:
-                pltpu.make_async_copy(buf.at[who], buf.at[who], recv_sem.at[b, who, 0]).wait()
-
-    started = {k: [] for k in range(4)}
-
-    def send(item, direction, plane):
-        pair = copies(item, direction, plane, len(started[plane]))
-        started[plane].append((item, direction))
+            piece = buf.at[who].at[:, pl.ds(part * half, half)]
+            pltpu.make_async_copy(piece, piece, recv_sem.at[b, who, part]).wait()
+
+    def send(event, plane):
+        pair = copies(event, plane, len(started[plane]))
+        started[plane].append(event)
         for copy in pair:
             copy.start()
 
     for plane in range(4):
         @pl.when(z == plane)
         def _(plane=plane):
-            dirs = {0: "uxy", 3: "vxy"}.get(plane, "uvxy")
-            for d in dirs:
-                send(("c", plane), d, plane)
+            for nth in range(2):
+                for d in {0: "xyu", 3: "xyv"}.get(plane, "uvxy"):
+                    send(("c", plane, 1 - nth if d == "y" else nth, d), plane)
 
     r_copy = pltpu.make_async_remote_copy(
         src_ref=right_in, dst_ref=rall.at[t], send_sem=r_send, recv_sem=r_recv,
@@ -227,6 +222,8 @@
     local[1].wait()
 
     ft = tile_of(ftotal, 16, 448)
+    tiles = ftotal // ft
+    pieces = p_send.shape[1] if tiles % p_send.shape[1] == 0 else 1
 
     def layer_index(step):
         ind = 0
@@ -234,7 +231,7 @@
             ind = ind + jnp.where(z == plane, ORDER[plane][step], 0)
         return ind
 
-    def compute(l, out_ref):
+    def compute(l):
         side = l % 2
         for i in range(4):
             lv = left[4 * l + i]
@@ -251,22 +248,37 @@
         )
         proj = jnp.where(mine, proj, 0.0).astype(jnp.bfloat16)
 
-        @pl.loop(0, ftotal // ft)
-        def _(i):
-            span = pl.ds(pl.multiple_of(i * ft, 16), ft)
-            value = lax.dot_general(
-                w[span, :], tok[pl.ds(4 * l, 4)].reshape(4 * rows, width), NT,
-                preferred_element_type=jnp.float32,
-            )
-            value = value + mixing * lax.dot_general(
-                rt_ref[span, :], proj, NT, preferred_element_type=jnp.float32
-            )
-            out_ref[side, span, :] = value.astype(jnp.bfloat16)
-
-    def exchange(side):
+        mine_here = l // 2 == t
+        for piece in range(pieces):
+            @pl.loop(piece * (tiles // pieces), (piece + 1) * (tiles // pieces))
+            def _(i):
+                span = pl.ds(pl.multiple_of(i * ft, 16), ft)
+                value = lax.dot_general(
+                    w[span, :], tok[pl.ds(4 * l, 4)].reshape(4 * rows, width), NT,
+                    preferred_element_type=jnp.float32,
+                )
+                value = value + mixing * lax.dot_general(
+                    rt_ref[span, :], proj, NT, preferred_element_type=jnp.float32
+                )
+                value = value.astype(jnp.bfloat16)
+
+                @pl.when(mine_here)
+                def _():
+                    own_ref[side, span, :] = value
+
+                @pl.when(jnp.logical_not(mine_here))
+                def _():
+                    sendb[side, span, :] = value
+
+            @pl.when(jnp.logical_not(mine_here))
+            def _():
+                exchange(side, piece).start()
+
+    def exchange(side, piece):
+        span = pl.ds(piece * (ftotal // pieces), ftotal // pieces)
         return pltpu.make_async_remote_copy(
-            src_ref=sendb.at[side], dst_ref=got_ref.at[side],
-            send_sem=p_send.at[side], recv_sem=p_recv.at[side],
+            src_ref=sendb.at[side].at[span], dst_ref=got_ref.at[side].at[span],
+            send_sem=p_send.at[side, piece], recv_sem=p_recv.at[side, piece],
             device_id=(m, 1 - t), device_id_type=MESH,
         )
 
@@ -274,48 +286,53 @@
         for plane in range(4):
             @pl.when(z == plane)
             def _(plane=plane, step=step):
-                for waits, sends in PLAN[plane][step]:
-                    for item in waits:
-                        await_item(item)
-                    for item, d in sends:
-                        send(item, d, plane)
-        l = layer_index(step)
+                for kind, l, part, dirs in PLAN[plane][step]:
+                    arrive(plane, kind, l, part)
+                    for d in dirs:
+                        send((kind, l, part, d), plane)
+                for kind in "cxyd":
+                    for part in range(2):
+                        arrive(plane, kind, ORDER[plane][step], part)
         if step == 0:
             local[3].wait()
-
-        @pl.when(l // 2 == t)
-        def _():
-            compute(l, own_ref)
-
-        @pl.when(l // 2 != t)
-        def _():
-            compute(l, sendb)
-            exchange(l % 2).start()
+        compute(layer_index(step))
 
     for plane in range(4):
         @pl.when(z == plane)
         def _(plane=plane):
-            for slot, (item, d) in enumerate(started[plane]):
-                for copy in copies(item, d, plane, slot):
+            for slot, event in enumerate(started[plane]):
+                for copy in copies(event, plane, slot):
                     copy.wait_send()
     for side in range(2):
-        exchange(side).wait()
-
-
-def finish_kernel(scale, facts, fit_ref, lpad_ref, rt_ref, own_ref, got_ref, h_ref, g_ref):
+        for piece in range(pieces):
+            exchange(side, piece).wait()
+
+
+def finish_kernel(scale, facts, fsteps, fit_ref, lpad_ref, rt_ref, own_ref, got_ref, h_ref, g_ref, wl):
     pad = lpad_ref.shape[0] // 16
-    rows = lax.broadcasted_iota(jnp.int32, (pad, 1), 0) // RANK
-    parts = []
-    for b in range(16):
-        col = jnp.zeros((pad, 1), jnp.float32)
-        for j in range(facts // RANK):
-            col = jnp.where(rows == j, fit_ref[b * (facts // RANK) + j], col)
-        parts.append((lpad_ref[pl.ds(b * pad, pad), :].astype(jnp.float32) * col).astype(jnp.bfloat16))
-    g = jnp.dot(rt_ref[...], jnp.concatenate(parts, axis=0), preferred_element_type=jnp.float32)
+    i, j = pl.program_id(0), pl.program_id(1)
+    tf, td = g_ref.shape
+
+    @pl.when(j == 0)
+    def _():
+        rows = lax.broadcasted_iota(jnp.int32, (pad, 1), 0) // RANK
+        span = pl.ds(pl.multiple_of(i * td, 128), td)
+        for b in range(16):
+            col = jnp.zeros((pad, 1), jnp.float32)
+            for r in range(facts // RANK):
+                col = jnp.where(rows == r, fit_ref[b * (facts // RANK) + r], col)
+            part = lpad_ref[pl.ds(b * pad, pad), span].astype(jnp.float32) * col
+            wl[pl.ds(b * pad, pad), :] = part.astype(jnp.bfloat16)
+
+    fspan = pl.ds(pl.multiple_of(j * tf, 16), tf)
+    g = jnp.dot(rt_ref[fspan, :], wl[...], preferred_element_type=jnp.float32)
     g_ref[...] = (g * scale).astype(jnp.bfloat16)
     n = own_ref.shape[2]
+    th = h_ref.shape[0]
+    at = jnp.minimum(i * pl.num_programs(1) + j, fsteps - 1)
+    hspan = pl.ds(pl.multiple_of(at * th, 16), th)
     for side in range(2):
-        total = own_ref[side].astype(jnp.float32) + got_ref[side].astype(jnp.float32)
+        total = own_ref[side, hspan, :].astype(jnp.float32) + got_ref[side, hspan, :].astype(jnp.float32)
         h_ref[:, side * n:(side + 1) * n] = total.astype(jnp.bfloat16)
 
 
@@ -332,7 +349,7 @@
     anyspec = pl.BlockSpec(memory_space=pltpu.HBM)
     vm = pl.BlockSpec(memory_space=pltpu.VMEM)
     dma = pltpu.SemaphoreType.DMA
-    nsend = 24
+    nsend = 40
     part = jax.ShapeDtypeStruct((2, columns, 4 * rows), bf)
     rt, lpad, own, got = pl.pallas_call(
         functools.partial(gather_kernel, mixing),
@@ -350,7 +367,7 @@
             pltpu.VMEM((columns, width), bf),
             pltpu.VMEM((2, rrows, columns), bf),
             pltpu.VMEM((2, columns, 4 * rows), bf),
-            dma((2, nsend)), dma((2, 16, 2)), dma((3,)), dma, dma, dma, dma((2,)), dma((2,)),
+            dma((2, nsend)), dma((2, 16, 2)), dma((3,)), dma, dma, dma, dma((2, 2)), dma((2, 2)),
         ],
         compiler_params=pltpu.CompilerParams(
             collective_id=0, has_side_effects=True, vmem_limit_bytes=40 * 1024 * 1024
@@ -363,28 +380,28 @@
         pltpu.with_memory_space_constraint(right_factors, pltpu.HBM),
     )
 
-    tf = tile_of(columns, 16, 192)
-    td = tile_of(width, 128, 256)
-    steps = max(width // td, columns // tf)
-    last_f, last_d = columns // tf - 1, width // td - 1
+    tf = tile_of(columns, 16, 1024)
+    td = tile_of(width, 128, 512)
+    dsteps, fsteps = width // td, columns // tf
+    th = columns
+    for size in range(16, columns, 16):
+        if columns % size == 0 and columns // size <= dsteps * fsteps:
+            th = size
+            break
+    last = columns // th - 1
     hidden, gradient = pl.pallas_call(
-        functools.partial(finish_kernel, 1.0 / (members * noise_scale * RANK**0.5), facts),
-        grid=(steps,),
+        functools.partial(finish_kernel, 1.0 / (members * noise_scale * RANK**0.5), facts, last + 1),
+        grid=(dsteps, fsteps),
         out_shape=(
             jax.ShapeDtypeStruct((columns, 8 * rows), bf),
             jax.ShapeDtypeStruct((columns, width), bf),
         ),
-        in_specs=[
-            pl.BlockSpec(memory_space=pltpu.SMEM),
-            pl.BlockSpec((16 * pad, td), lambda i: (0, jnp.minimum(i, last_d))),
-            pl.BlockSpec((columns, 16 * pad), lambda i: (0, 0)),
-            pl.BlockSpec((2, tf, 4 * rows), lambda i: (0, jnp.minimum(i, last_f), 0)),
-            pl.BlockSpec((2, tf, 4 * rows), lambda i: (0, jnp.minimum(i, last_f), 0)),
-        ],
+        in_specs=[pl.BlockSpec(memory_space=pltpu.SMEM), vm, vm, vm, vm],
         out_specs=(
-            pl.BlockSpec((tf, 8 * rows), lambda i: (jnp.minimum(i, last_f), 0)),
-            pl.BlockSpec((columns, td), lambda i: (0, jnp.minimum(i, last_d))),
+            pl.BlockSpec((th, 8 * rows), lambda i, j: (jnp.minimum(i * fsteps + j, last), 0)),
+            pl.BlockSpec((tf, td), lambda i, j: (j, i)),
         ),
+        scratch_shapes=[pltpu.VMEM((16 * pad, td), bf)],
         compiler_params=pltpu.CompilerParams(vmem_limit_bytes=24 * 1024 * 1024),
         name="finish",
     )(fitness, lpad, rt, own, got)

time: 60.1 us -> 58.2 us (0.968)
  Pallas kernels: 59.3 us -> 57.3 us
    pallas_call x1, Pallas kernels: 51.4 us -> 49.5 us  [body(): pl.pallas_call(functools.partial(gather_kernel, mixing), out_shape=(jax.S...]
where the time goes in v3:
time: 58.2 us; the launch traced here: 58 us
  Pallas kernels  57.3 us (98%)
  between operations  0.65 us (1%)
    pallas_call x1, Pallas kernels, body(): pl.pallas_call(functools.partial(gather_kernel, mixing), out_shape=(jax.S...  49.5 us
    pallas_call x1, Pallas kernels, body(): pl.pallas_call(functools.partial(finish_kernel, 1.0 / (members * noise_sc...  7.89 us

profile of v3, /device:TPU:0, one launch (start us, length us, event | category | flops | bytes accessed | tf_op | source)
XLA Modules:
  0.0 58.0 jit_solution(7163316886980078187)
XLA Ops:
  0.6 0.0 copy-start
  0.6 49.5 %gather_project.1 = (bf16[1728,256]{1,0:T(8,128)(2,1)S(1)}, bf16[256,2560]{1,0:T(8,128)(2,1)S(1)}, bf16[2,1728,192]{2,1,0:T(8,128)(2,1)S(1)}, bf16[2,1728,192]{2,1,0:T(8,128)(2,1)S(1)}) custom-call(bf16[48,2560]{1,0:T(8,128)(2,1)} %tok_in.1, bf16[1728,2560]{1,0:T(8,128)(2,1)} %bitcast.3, bf16[12,2560]{1,0:T(8,128)(2,1)} %left_in.1, bf16[96,1728]{1,0:T(8,128)(2,1)} %right_in.1), custom_call_target="tpu_custom_call" | custom-call | tf_op jit(solution)/shard_map/gather_project/pallas_call | solution.py:354
  50.1 0.0 copy-done
  50.1 7.9 %finish.1 = (bf16[1728,384]{1,0:T(8,128)(2,1)}, bf16[1728,2560]{1,0:T(8,128)(2,1)}) custom-call(f32[48]{0:T(128)S(1)} %copy-done, bf16[256,2560]{1,0:T(8,128)(2,1)S(1)} %get-tuple-element.8.lpad_ref, bf16[1728,256]{1,0:T(8,128)(2,1)S(1)} %get-tuple-element.9.rt_ref, bf16[2,1728,192]{2,1,0:T(8,128)(2,1)S(1)} %get-tuple-element.10.own_ref, ...), custom_call_target="tpu_custom_call" | custom-call | tf_op jit(solution)/shard_map/finish/pallas_call | solution.py:392
Async XLA Ops:
  0.6 49.5 %copy-start = (f32[48]{0:T(128)S(1)}, f32[48]{0:T(128)}, u32[]{:S(2)}) copy-start(f32[48]{0:T(128)} %fit_ref.1) | copy-start | bytes 580

commit v4 on v3

--- a/solution.py
+++ b/solution.py
@@ -308,32 +308,41 @@
             exchange(side, piece).wait()
 
 
-def finish_kernel(scale, facts, fsteps, fit_ref, lpad_ref, rt_ref, own_ref, got_ref, h_ref, g_ref, wl):
+def finish_kernel(
+    scale, facts, tf, td, th, fit_ref, lpad_ref, rt_ref, own_ref, got_ref,
+    h_ref, g_ref, wl, gbuf, hbuf, g_sem, h_sem,
+):
     pad = lpad_ref.shape[0] // 16
-    i, j = pl.program_id(0), pl.program_id(1)
-    tf, td = g_ref.shape
-
-    @pl.when(j == 0)
-    def _():
-        rows = lax.broadcasted_iota(jnp.int32, (pad, 1), 0) // RANK
-        span = pl.ds(pl.multiple_of(i * td, 128), td)
+    columns, width = gbuf.shape
+    n = own_ref.shape[2]
+    rows = lax.broadcasted_iota(jnp.int32, (pad, 1), 0) // RANK
+    copies = []
+    slices = columns // th
+    for i in range(width // td):
+        span = pl.ds(i * td, td)
         for b in range(16):
             col = jnp.zeros((pad, 1), jnp.float32)
             for r in range(facts // RANK):
                 col = jnp.where(rows == r, fit_ref[b * (facts // RANK) + r], col)
             part = lpad_ref[pl.ds(b * pad, pad), span].astype(jnp.float32) * col
-            wl[pl.ds(b * pad, pad), :] = part.astype(jnp.bfloat16)
-
-    fspan = pl.ds(pl.multiple_of(j * tf, 16), tf)
-    g = jnp.dot(rt_ref[fspan, :], wl[...], preferred_element_type=jnp.float32)
-    g_ref[...] = (g * scale).astype(jnp.bfloat16)
-    n = own_ref.shape[2]
-    th = h_ref.shape[0]
-    at = jnp.minimum(i * pl.num_programs(1) + j, fsteps - 1)
-    hspan = pl.ds(pl.multiple_of(at * th, 16), th)
-    for side in range(2):
-        total = own_ref[side, hspan, :].astype(jnp.float32) + got_ref[side, hspan, :].astype(jnp.float32)
-        h_ref[:, side * n:(side + 1) * n] = total.astype(jnp.bfloat16)
+            wl[pl.ds(b * pad, pad), span] = part.astype(jnp.bfloat16)
+        for j in range(columns // tf):
+            nth = i * (columns // tf) + j
+            fspan = pl.ds(j * tf, tf)
+            g = jnp.dot(rt_ref[fspan, :], wl[:, span], preferred_element_type=jnp.float32)
+            gbuf[fspan, span] = (g * scale).astype(jnp.bfloat16)
+            copies.append(pltpu.make_async_copy(gbuf.at[fspan, span], g_ref.at[fspan, span], g_sem.at[nth]))
+            copies[-1].start()
+            if nth < slices:
+                hspan = pl.ds(nth * th, th)
+                for side in range(2):
+                    total = own_ref[side, hspan, :].astype(jnp.float32)
+                    total = total + got_ref[side, hspan, :].astype(jnp.float32)
+                    hbuf[hspan, side * n:(side + 1) * n] = total.astype(jnp.bfloat16)
+                copies.append(pltpu.make_async_copy(hbuf.at[hspan], h_ref.at[hspan], h_sem.at[nth]))
+                copies[-1].start()
+    for copy in copies:
+        copy.wait()
 
 
 def body(tokens, up_weight, left_factors, right_factors, fitness):
@@ -380,28 +389,31 @@
         pltpu.with_memory_space_constraint(right_factors, pltpu.HBM),
     )
 
-    tf = tile_of(columns, 16, 1024)
+    tf = tile_of(columns, 16, 448)
     td = tile_of(width, 128, 512)
-    dsteps, fsteps = width // td, columns // tf
+    tiles = (columns // tf) * (width // td)
     th = columns
     for size in range(16, columns, 16):
-        if columns % size == 0 and columns // size <= dsteps * fsteps:
+        if columns % size == 0 and columns // size <= tiles:
             th = size
             break
-    last = columns // th - 1
     hidden, gradient = pl.pallas_call(
-        functools.partial(finish_kernel, 1.0 / (members * noise_scale * RANK**0.5), facts, last + 1),
-        grid=(dsteps, fsteps),
+        functools.partial(
+            finish_kernel, 1.0 / (members * noise_scale * RANK**0.5), facts, tf, td, th
+        ),
         out_shape=(
             jax.ShapeDtypeStruct((columns, 8 * rows), bf),
             jax.ShapeDtypeStruct((columns, width), bf),
         ),
         in_specs=[pl.BlockSpec(memory_space=pltpu.SMEM), vm, vm, vm, vm],
-        out_specs=(
-            pl.BlockSpec((th, 8 * rows), lambda i, j: (jnp.minimum(i * fsteps + j, last), 0)),
-            pl.BlockSpec((tf, td), lambda i, j: (j, i)),
-        ),
-        scratch_shapes=[pltpu.VMEM((16 * pad, td), bf)],
+        out_specs=(anyspec, anyspec),
+        scratch_shapes=[
+            pltpu.VMEM((16 * pad, width), bf),
+            pltpu.VMEM((columns, width), bf),
+            pltpu.VMEM((columns, 8 * rows), bf),
+            dma((tiles,)),
+            dma((columns // th,)),
+        ],
         compiler_params=pltpu.CompilerParams(vmem_limit_bytes=24 * 1024 * 1024),
         name="finish",
     )(fitness, lpad, rt, own, got)

time: 58.2 us -> 55.3 us (0.950)
  Pallas kernels: 57.3 us -> 54.5 us
    pallas_call x1, Pallas kernels: 7.89 us -> 5 us  [body(): pl.pallas_call(functools.partial(finish_kernel, 1.0 / (members * noise_sc...]
where the time goes in v4:
time: 55.3 us; the launch traced here: 55.1 us
  Pallas kernels  54.5 us (99%)
  between operations  0.65 us (1%)
    pallas_call x1, Pallas kernels, body(): pl.pallas_call(functools.partial(gather_kernel, mixing), out_shape=(jax.S...  49.5 us
    pallas_call x1, Pallas kernels, body(): pl.pallas_call(functools.partial(finish_kernel, 1.0 / (members * noise_sc...  5 us

profile of v4, /device:TPU:0, one launch (start us, length us, event | category | flops | bytes accessed | tf_op | source)
XLA Modules:
  0.0 55.1 jit_solution(13926036979211680875)
XLA Ops:
  0.6 0.0 copy-start
  0.6 49.5 %gather_project.1 = (bf16[1728,256]{1,0:T(8,128)(2,1)S(1)}, bf16[256,2560]{1,0:T(8,128)(2,1)S(1)}, bf16[2,1728,192]{2,1,0:T(8,128)(2,1)S(1)}, bf16[2,1728,192]{2,1,0:T(8,128)(2,1)S(1)}) custom-call(bf16[48,2560]{1,0:T(8,128)(2,1)} %tok_in.1, bf16[1728,2560]{1,0:T(8,128)(2,1)} %bitcast.3, bf16[12,2560]{1,0:T(8,128)(2,1)} %left_in.1, bf16[96,1728]{1,0:T(8,128)(2,1)} %right_in.1), custom_call_target="tpu_custom_call" | custom-call | tf_op jit(solution)/shard_map/gather_project/pallas_call | solution.py:363
  50.1 0.0 copy-done
  50.1 5.0 %finish.1 = (bf16[1728,384]{1,0:T(8,128)(2,1)}, bf16[1728,2560]{1,0:T(8,128)(2,1)}) custom-call(f32[48]{0:T(128)S(1)} %copy-done, bf16[256,2560]{1,0:T(8,128)(2,1)S(1)} %get-tuple-element.8.lpad_ref, bf16[1728,256]{1,0:T(8,128)(2,1)S(1)} %get-tuple-element.9.rt_ref, bf16[2,1728,192]{2,1,0:T(8,128)(2,1)S(1)} %get-tuple-element.10.own_ref, ...), custom_call_target="tpu_custom_call" | custom-call | tf_op jit(solution)/shard_map/finish/pallas_call | solution.py:400
Async XLA Ops:
  0.6 49.5 %copy-start = (f32[48]{0:T(128)S(1)}, f32[48]{0:T(128)}, u32[]{:S(2)}) copy-start(f32[48]{0:T(128)} %fit_ref.1) | copy-start | bytes 580
